TPU v7x, 32 devices: a whole 2x2x4 slice. The times are simulated.
32 devices in a mesh: dp: 8 (over z, core), tensor: 4 (over y, x).
Axes of the slice: x: 2, y: 2, z: 4, core: 2. Of those that a mesh axis runs over, the one named last changes fastest.
Arguments:
- byte_in: bfloat16 [32, 4096, 768], P('dp', 'tensor'), may hold values from -6 to 6
- lengths: int32 [32], P('dp'), may hold values from 1024 to 4096, as said below
- latent: bfloat16 [256, 1280], P('tensor', 'dp'), may hold values from -6 to 6
- g_in: float32 [768], replicated, may hold values from 0.1 to 1.9
- b_in: float32 [768], replicated, may hold values from -3 to 3
- g_lat: float32 [1280], replicated, may hold values from 0.1 to 1.9
- b_lat: float32 [1280], replicated, may hold values from -3 to 3
- w_query: bfloat16 [1280, 256], P('dp', 'tensor'), may hold values from -0.15625 to 0.15625
- w_key: bfloat16 [768, 256], P('dp', 'tensor'), may hold values from -0.21875 to 0.21875
- w_value: bfloat16 [768, 1280], P('dp', 'tensor'), may hold values from -0.21875 to 0.21875
- w_out: bfloat16 [1280, 1280], P('tensor', 'dp'), may hold values from -6 to 6
- g_mlp: float32 [1280], replicated, may hold values from 0.1 to 1.9
- b_mlp: float32 [1280], replicated, may hold values from -3 to 3
- w_hidden: bfloat16 [1280, 1280], P('dp', 'tensor'), may hold values from -0.15625 to 0.15625
- b_hidden: float32 [1280], replicated, may hold values from -3 to 3
- w_back: bfloat16 [1280, 1280], P('tensor', 'dp'), may hold values from -0.15625 to 0.15625
- b_back: float32 [1280], replicated, may hold values from -3 to 3
- cotangent: float32 [32, 256, 1280], P('dp', 'tensor'), may hold values from -6 to 6
Outputs:
- latents_out: float32 [32, 256, 1280], P('dp', 'tensor')
- grad_bytes: float32 [32, 4096, 768], P('dp', 'tensor')
- grad_latent: float32 [256, 1280], P('tensor', 'dp')
- grad_g_in: float32 [768], replicated
- grad_b_in: float32 [768], replicated
- grad_g_lat: float32 [1280], replicated
- grad_b_lat: float32 [1280], replicated
- grad_w_query: float32 [1280, 256], P('dp', 'tensor')
- grad_w_key: float32 [768, 256], P('dp', 'tensor')
- grad_w_value: float32 [768, 1280], P('dp', 'tensor')
- grad_w_out: float32 [1280, 1280], P('tensor', 'dp')
- grad_g_mlp: float32 [1280], replicated
- grad_b_mlp: float32 [1280], replicated
- grad_w_hidden: float32 [1280, 1280], P('dp', 'tensor')
- grad_b_hidden: float32 [1280], replicated
- grad_w_back: float32 [1280, 1280], P('tensor', 'dp')
- grad_b_back: float32 [1280], replicated
Inputs may be any that keep to these rules, and one draw needn't show every extreme that they name: Sequence b has live bytes at slots below lengths[b] and padding from there on; the first sequence is full.
All inputs are finite; a program needn't handle non-finite values.
Results may differ from a plain program's by a relative error of at most 0.019.
Values may be sent and summed in bfloat16 or wider, within the bound.
No kernel may reach another device: no remote copies, remote signals or barrier semaphores. Data moves between devices by JAX's collectives and lax.ppermute only.
A program may use at most 256 MiB of HBM per device.

v0:
```python
from functools import partial
import jax
import jax.numpy as jnp
from jax import lax
from jax.sharding import PartitionSpec as P

HQ = 32
HV = 160
NEGATIVE = -1e30


def normalize(values, gain, shift):
    center = jnp.mean(values, axis=-1, keepdims=True)
    centered = values - center
    spread = jnp.mean(centered * centered, axis=-1, keepdims=True)
    return centered * lax.rsqrt(spread + 1e-05) * gain + shift


def norm_backward(values, gain, shift, upstream):
    normed, pullback = jax.vjp(normalize, values, gain, shift)
    return pullback(upstream)


def exact_gelu(values):
    return jax.nn.gelu(values, approximate=False)


def head_scores(query_all, keys_seq, length):
    heads = query_all.shape[1] // HQ
    query_heads = query_all.reshape(query_all.shape[0], heads, HQ)
    key_heads = keys_seq.reshape(keys_seq.shape[0], heads, HQ)
    raw = jnp.einsum("nhd,lhd->hnl", query_heads, key_heads, preferred_element_type=jnp.float32)
    live = lax.iota(jnp.int32, keys_seq.shape[0]) < length
    return jnp.where(live[None, None, :], raw * HQ ** (-0.5), NEGATIVE)


def attend_forward(query_all, item):
    keys_seq, values_seq, length = item
    scores = head_scores(query_all, keys_seq, length)
    summit = jnp.max(scores, axis=-1, keepdims=True)
    weights = jnp.exp(scores - summit)
    total = jnp.sum(weights, axis=-1, keepdims=True)
    probs = weights / total
    heads = scores.shape[0]
    value_heads = values_seq.reshape(values_seq.shape[0], heads, HV)
    mixed = jnp.einsum(
        "hnl,lhe->nhe", probs.astype(jnp.bfloat16), value_heads, preferred_element_type=jnp.float32
    )
    mixed = mixed.reshape(mixed.shape[0], heads * HV).astype(jnp.bfloat16)
    return (mixed, (summit + jnp.log(total))[..., 0])


def score_backward(query_all, keys_seq, values_seq, probs, grad_mixed, inner):
    heads = probs.shape[0]
    latents = query_all.shape[0]
    slots = keys_seq.shape[0]
    value_heads = values_seq.reshape(slots, heads, HV)
    grad_heads = grad_mixed.reshape(latents, heads, HV)
    grad_probs = jnp.einsum(
        "nhe,lhe->hnl", grad_heads, value_heads, preferred_element_type=jnp.float32
    )
    grad_values = jnp.einsum(
        "hnl,nhe->lhe", probs.astype(jnp.bfloat16), grad_heads, preferred_element_type=jnp.float32
    )
    inner = jnp.sum(probs * grad_probs, axis=-1, keepdims=True)
    grad_scores = (probs * (grad_probs - inner) * HQ ** (-0.5)).astype(jnp.bfloat16)
    query_heads = query_all.reshape(latents, heads, HQ)
    key_heads = keys_seq.reshape(slots, heads, HQ)
    grad_query = jnp.einsum(
        "hnl,lhd->nhd", grad_scores, key_heads, preferred_element_type=jnp.float32
    )
    grad_keys = jnp.einsum(
        "hnl,nhd->lhd", grad_scores, query_heads, preferred_element_type=jnp.float32
    )
    return (
        grad_query.reshape(latents, heads * HQ),
        grad_keys.reshape(slots, heads * HQ).astype(jnp.bfloat16),
        grad_values.reshape(slots, heads * HV).astype(jnp.bfloat16),
    )


def rows_backward(query_all, item):
    keys_seq, values_seq, length, log_total, grad_mixed = item
    scores = head_scores(query_all, keys_seq, length)
    probs = jnp.exp(scores - log_total[..., None])
    return score_backward(query_all, keys_seq, values_seq, probs, grad_mixed, None)


def on_device(
    byte_in,
    lengths,
    latent,
    g_in,
    b_in,
    g_lat,
    b_lat,
    w_query,
    w_key,
    w_value,
    w_out,
    g_mlp,
    b_mlp,
    w_hidden,
    b_hidden,
    w_back,
    b_back,
    cotangent,
):
    full_query, full_key, full_value, full_hidden, full_out, full_back, latent_rows = (
        lax.all_gather(w_query, "dp", axis=0, tiled=True),
        lax.all_gather(w_key, "dp", axis=0, tiled=True),
        lax.all_gather(w_value, "dp", axis=0, tiled=True),
        lax.all_gather(w_hidden, "dp", axis=0, tiled=True),
        lax.all_gather(w_out, "dp", axis=1, tiled=True),
        lax.all_gather(w_back, "dp", axis=1, tiled=True),
        lax.all_gather(latent, "dp", axis=1, tiled=True),
    )
    tensor_rank = lax.axis_index("tensor")
    latent_float = latent_rows.astype(jnp.float32)
    latent_norm = normalize(latent_float, g_lat, b_lat).astype(jnp.bfloat16)
    byte_float = byte_in.astype(jnp.float32)
    byte_norm = normalize(byte_float, g_in, b_in).astype(jnp.bfloat16)
    latent_all, byte_all = (
        lax.all_gather(latent_norm, "tensor", axis=0, tiled=True),
        lax.all_gather(byte_norm, "tensor", axis=1, tiled=True),
    )
    keys = jnp.einsum("slc,cq->slq", byte_all, full_key, preferred_element_type=jnp.float32).astype(
        jnp.bfloat16
    )
    values = jnp.einsum(
        "slc,cv->slv", byte_all, full_value, preferred_element_type=jnp.float32
    ).astype(jnp.bfloat16)
    query = jnp.dot(latent_all, full_query, preferred_element_type=jnp.float32).astype(jnp.bfloat16)
    mixed, log_totals = lax.map(partial(attend_forward, query), (keys, values, lengths))
    attn_term = jnp.einsum("snv,vd->snd", mixed, full_out, preferred_element_type=jnp.float32)
    attn_rows = lax.psum_scatter(attn_term, "tensor", scatter_dimension=1, tiled=True)
    middle = latent_float[None] + attn_rows
    hidden_norm = normalize(middle, g_mlp, b_mlp).astype(jnp.bfloat16)
    out_grad = cotangent.astype(jnp.bfloat16)
    hidden_all, out_grad_all = (
        lax.all_gather(hidden_norm, "tensor", axis=1, tiled=True),
        lax.all_gather(out_grad, "tensor", axis=1, tiled=True),
    )
    width = full_hidden.shape[1]
    offset = tensor_rank * width
    bias_part = lax.dynamic_slice_in_dim(b_hidden, offset, width)
    pre = (
        jnp.einsum("snd,df->snf", hidden_all, full_hidden, preferred_element_type=jnp.float32)
        + bias_part
    )
    activation, gelu_pull = jax.vjp(exact_gelu, pre)
    act_low = activation.astype(jnp.bfloat16)
    branch_term = jnp.einsum("snf,fd->snd", act_low, full_back, preferred_element_type=jnp.float32)
    branch_rows = lax.psum_scatter(
        branch_term.astype(jnp.bfloat16), "tensor", scatter_dimension=1, tiled=True
    ).astype(jnp.float32)
    latents_out = middle + branch_rows + b_back
    grad_back_part = jnp.einsum(
        "snf,snd->fd", act_low, out_grad_all, preferred_element_type=jnp.float32
    )
    grad_act = jnp.einsum(
        "snd,fd->snf", out_grad_all, full_back, preferred_element_type=jnp.float32
    )
    grad_pre = gelu_pull(grad_act)[0].astype(jnp.bfloat16)
    grad_bias_part = jnp.sum(grad_pre.astype(jnp.float32), axis=(0, 1))
    grad_hidden_part = jnp.einsum(
        "snd,snf->df", hidden_all, grad_pre, preferred_element_type=jnp.float32
    )
    hidden_term = jnp.einsum(
        "snf,df->snd", grad_pre, full_hidden, preferred_element_type=jnp.float32
    )
    grad_hidden = lax.psum_scatter(hidden_term, "tensor", scatter_dimension=1, tiled=True)
    grad_mid_norm, grad_g_mlp, grad_b_mlp = norm_backward(middle, g_mlp, b_mlp, grad_hidden)
    grad_middle = cotangent + grad_mid_norm
    middle_low = grad_middle.astype(jnp.bfloat16)
    middle_all = lax.all_gather(middle_low, "tensor", axis=1, tiled=True)
    grad_out_part = jnp.einsum("snv,snd->vd", mixed, middle_all, preferred_element_type=jnp.float32)
    grad_mixed = jnp.einsum(
        "snd,vd->snv", middle_all, full_out, preferred_element_type=jnp.float32
    ).astype(jnp.bfloat16)
    query_parts, grad_keys, grad_values = lax.map(
        partial(rows_backward, query), (keys, values, lengths, log_totals, grad_mixed)
    )
    grad_query = query_parts.astype(jnp.bfloat16)
    grad_query_part = jnp.einsum(
        "nd,snq->dq", latent_all, grad_query, preferred_element_type=jnp.float32
    )
    latent_term = jnp.einsum(
        "snq,dq->nd", grad_query, full_query, preferred_element_type=jnp.float32
    )
    grad_key_part = jnp.einsum(
        "slc,slq->cq", byte_all, grad_keys, preferred_element_type=jnp.float32
    )
    grad_value_part = jnp.einsum(
        "slc,slv->cv", byte_all, grad_values, preferred_element_type=jnp.float32
    )
    byte_term = jnp.einsum("slq,cq->slc", grad_keys, full_key, preferred_element_type=jnp.float32)
    byte_term = byte_term + jnp.einsum(
        "slv,cv->slc", grad_values, full_value, preferred_element_type=jnp.float32
    )
    grad_latent_norm, grad_byte_norm = (
        lax.psum_scatter(
            latent_term.astype(jnp.bfloat16), "tensor", scatter_dimension=0, tiled=True
        ).astype(jnp.float32),
        lax.psum_scatter(
            byte_term.astype(jnp.bfloat16), "tensor", scatter_dimension=1, tiled=True
        ).astype(jnp.float32),
    )
    grad_bytes, grad_g_in, grad_b_in = norm_backward(byte_float, g_in, b_in, grad_byte_norm)
    grad_lat_rows, grad_g_lat, grad_b_lat = norm_backward(
        latent_float, g_lat, b_lat, grad_latent_norm
    )
    latent_part = grad_lat_rows + jnp.sum(grad_middle, axis=0)
    grad_w_query, grad_w_key, grad_w_value, grad_w_hidden, grad_w_out, grad_w_back, grad_latent = (
        lax.psum_scatter(
            grad_query_part.astype(jnp.bfloat16), "dp", scatter_dimension=0, tiled=True
        ).astype(jnp.float32),
        lax.psum_scatter(
            grad_key_part.astype(jnp.bfloat16), "dp", scatter_dimension=0, tiled=True
        ).astype(jnp.float32),
        lax.psum_scatter(
            grad_value_part.astype(jnp.bfloat16), "dp", scatter_dimension=0, tiled=True
        ).astype(jnp.float32),
        lax.psum_scatter(
            grad_hidden_part.astype(jnp.bfloat16), "dp", scatter_dimension=0, tiled=True
        ).astype(jnp.float32),
        lax.psum_scatter(
            grad_out_part.astype(jnp.bfloat16), "dp", scatter_dimension=1, tiled=True
        ).astype(jnp.float32),
        lax.psum_scatter(
            grad_back_part.astype(jnp.bfloat16), "dp", scatter_dimension=1, tiled=True
        ).astype(jnp.float32),
        lax.psum_scatter(
            latent_part.astype(jnp.bfloat16), "dp", scatter_dimension=1, tiled=True
        ).astype(jnp.float32),
    )
    bias_full = lax.dynamic_update_slice_in_dim(
        jnp.zeros(b_hidden.shape, jnp.float32), grad_bias_part, offset, 0
    )
    back_bias = jnp.sum(cotangent, axis=(0, 1))
    (
        sum_g_in,
        sum_b_in,
        sum_g_lat,
        sum_b_lat,
        sum_g_mlp,
        sum_b_mlp,
        sum_hidden_bias,
        sum_back_bias,
    ) = lax.psum(
        (
            grad_g_in,
            grad_b_in,
            grad_g_lat,
            grad_b_lat,
            grad_g_mlp,
            grad_b_mlp,
            bias_full,
            back_bias,
        ),
        ("dp", "tensor"),
    )
    return (
        latents_out,
        grad_bytes,
        grad_latent,
        sum_g_in,
        sum_b_in,
        sum_g_lat,
        sum_b_lat,
        grad_w_query,
        grad_w_key,
        grad_w_value,
        grad_w_out,
        sum_g_mlp,
        sum_b_mlp,
        grad_w_hidden,
        sum_hidden_bias,
        grad_w_back,
        sum_back_bias,
    )


def solution(mesh):
    return jax.shard_map(
        on_device,
        mesh=mesh,
        in_specs=(
            P("dp", "tensor", None),
            P("dp"),
            P("tensor", "dp"),
            P(),
            P(),
            P(),
            P(),
            P("dp", "tensor"),
            P("dp", "tensor"),
            P("dp", "tensor"),
            P("tensor", "dp"),
            P(),
            P(),
            P("dp", "tensor"),
            P(),
            P("tensor", "dp"),
            P(),
            P("dp", "tensor", None),
        ),
        out_specs=(
            P("dp", "tensor", None),
            P("dp", "tensor", None),
            P("tensor", "dp"),
            P(),
            P(),
            P(),
            P(),
            P("dp", "tensor"),
            P("dp", "tensor"),
            P("dp", "tensor"),
            P("tensor", "dp"),
            P(),
            P(),
            P("dp", "tensor"),
            P(),
            P("tensor", "dp"),
            P(),
        ),
        check_vma=False,
    )
```

profile of v0, /device:TPU:0, one launch (start us, length us, event | category | flops | bytes accessed | tf_op | source)
XLA Modules:
  0.0 1378.6 jit_solution(1738117160215363576)
XLA Ops:
  7.2 3.8 convert_reduce_fusion.1
  15.0 4.3 fusion.22
  20.0 15.7 %all-gather.1 = bf16[8,96,64]{1,2,0:T(8,128)(2,1)S(1)} all-gather(bf16[1,96,64]{1,2,0:T(8,128)(2,1)S(1)} %bitcast.266), channel_id=1, replica_groups=mesh['dp'=8,'tensor'=4] {'dp'}, dimensions={0}, use_global_device_ids=true | all-gather | bytes 110592 | tf_op jit(solution)/shard_map/all_gather | solution.py:111
  36.0 14.2 %all-gather = bf16[8,160,64]{1,2,0:T(8,128)(2,1)S(1)} all-gather(bf16[1,160,64]{1,2,0:T(8,128)(2,1)S(1)} %bitcast.264), channel_id=1, replica_groups=mesh['dp'=8,'tensor'=4] {'dp'}, dimensions={0}, use_global_device_ids=true | all-gather | bytes 184320 | tf_op jit(solution)/shard_map/all_gather | solution.py:116
  50.6 14.2 %all-gather.2 = bf16[8,160,64]{1,2,0:T(8,128)(2,1)S(1)} all-gather(bf16[1,160,64]{1,2,0:T(8,128)(2,1)S(1)} %bitcast.265), channel_id=1, replica_groups=mesh['dp'=8,'tensor'=4] {'dp'}, dimensions={0}, use_global_device_ids=true | all-gather | bytes 184320 | tf_op jit(solution)/shard_map/all_gather | solution.py:110
  65.7 17.8 %all_gather.40 = bf16[256,1280]{1,0:T(8,128)(2,1)S(1)} all-gather(bf16[64,1280]{1,0:T(8,128)(2,1)S(1)} %add_convert_fusion.4), channel_id=1, replica_groups=mesh['dp'=8,'tensor'=4] {'tensor'}, dimensions={0}, use_global_device_ids=true | all-gather | bytes 819200 | tf_op jit(solution)/shard_map/all_gather | solution.py:124
  83.6 16.1 %all_gather.38 = bf16[768,320]{1,0:T(8,128)(2,1)} all-gather(bf16[96,320]{1,0:T(8,128)(2,1)S(1)} %copy-done.30), channel_id=1, replica_groups=mesh['dp'=8,'tensor'=4] {'dp'}, dimensions={0}, use_global_device_ids=true | all-gather | bytes 552960 | tf_op jit(solution)/shard_map/all_gather | solution.py:112
  100.0 17.1 %all_gather.42 = bf16[320,1280]{0,1:T(8,128)(2,1)S(1)} all-gather(bf16[320,160]{0,1:T(8,128)(2,1)S(1)} %copy-done.26), channel_id=1, replica_groups=mesh['dp'=8,'tensor'=4] {'dp'}, dimensions={1}, use_global_device_ids=true | all-gather | bytes 921600 | tf_op jit(solution)/shard_map/all_gather | solution.py:114
  117.1 137.7 %all-gather.8.cloned.1.call-done = bf16[4,4096,768]{2,1,0:T(8,128)(2,1)} async-done(((bf16[4,1024,768]{2,1,0:T(8,128)(2,1)}), bf16[4,4096,768]{2,1,0:T(8,128)(2,1)}) %all-gather.8.cloned.1.call-update) | async-done | bytes 25165840 | tf_op jit(solution)/shard_map/all_gather | solution.py:125
  254.8 15.8 %convolution_convert_fusion.3 = bf16[4,4096,64]{1,2,0:T(8,128)(2,1)S(1)} fusion(bf16[4,4096,768]{2,1,0:T(8,128)(2,1)} %all-gather.8.cloned.1.call-done, bf16[768,64,1]{0,1,2:T(8,128)(2,1)S(1)} %reshape.241), kind=kOutput, calls=%fused_computation.59 | convolution fusion | flops 1611661312 | bytes 27361280 | tf_op jit(solution)/shard_map/slc,cq->slq/dot_general | solution.py:127
  270.7 17.0 %convolution_convert_fusion.2 = bf16[4,4096,320]{1,2,0:T(8,128)(2,1)} fusion(bf16[4,4096,768]{2,1,0:T(8,128)(2,1)} %all-gather.8.cloned.1.call-done, bf16[768,320]{1,0:T(8,128)(2,1)S(1)} %copy-done.9), kind=kOutput, calls=%fused_computation.56 | convolution fusion | flops 8058306560 | bytes 36143104 | tf_op jit(solution)/shard_map/slc,cv->slv/dot_general | solution.py:130
  287.7 50.4 %while.26 = (s32[]{:T(128)}, bf16[4,256,320]{1,2,0:T(8,128)(2,1)}, f32[4,2,256]{2,1,0:T(2,128)S(1)}, bf16[4,4096,320]{1,2,0:T(8,128)(2,1)}, s32[4]{0:T(128)S(1)}...) while((s32[]{:T(128)}, bf16[4,256,320]{1,2,0:T(8,128)(2,1)}, ...), condition=%wide.region_7.8_spmd, body=%wide.region_4.7_spmd.sunk | while | flops 830557696 | bytes 35160188 | solution.py:134
  291.0 3.6 bitcast_reduce_fusion.2
  303.6 3.6 bitcast_reduce_fusion.2
  316.2 3.6 bitcast_reduce_fusion.2
  328.8 3.6 bitcast_reduce_fusion.2
  338.1 5.4 fusion.45
  343.6 61.5 %reduce-scatter.19.cloned.1.call-done = f32[4,64,1280]{2,1,0:T(8,128)} async-done(((f32[4,256,1280]{2,1,0:T(8,128)}), f32[4,64,1280]{2,1,0:T(8,128)}) %reduce-scatter.19.cloned.1.call-update) | async-done | bytes 1310736 | tf_op jit(solution)/shard_map/reduce_scatter | solution.py:136
  410.2 17.2 %all_gather.44 = bf16[1280,320]{1,0:T(8,128)(2,1)} all-gather(bf16[160,320]{1,0:T(8,128)(2,1)S(1)} %copy-done.27), channel_id=1, replica_groups=mesh['dp'=8,'tensor'=4] {'dp'}, dimensions={0}, use_global_device_ids=true | all-gather | bytes 921600 | tf_op jit(solution)/shard_map/all_gather | solution.py:113
  427.3 17.5 %all_gather.45 = bf16[320,1280]{0,1:T(8,128)(2,1)} all-gather(bf16[320,160]{0,1:T(8,128)(2,1)S(1)} %copy-done.28), channel_id=1, replica_groups=mesh['dp'=8,'tensor'=4] {'dp'}, dimensions={1}, use_global_device_ids=true | all-gather | bytes 921600 | tf_op jit(solution)/shard_map/all_gather | solution.py:115
  448.1 3.4 fusion.57
  452.6 4.1 multiply_convert_fusion
  456.6 32.9 %all-gather.12.cloned.1.call-done = bf16[4,256,1280]{2,1,0:T(8,128)(2,1)} async-done(((bf16[4,64,1280]{2,1,0:T(8,128)(2,1)}), bf16[4,256,1280]{2,1,0:T(8,128)(2,1)}) %all-gather.12.cloned.1.call-update) | async-done | bytes 2621456 | tf_op jit(solution)/shard_map/all_gather | solution.py:142
  489.5 5.0 convert_reduce_fusion.2
  495.3 3.9 fusion.41
  499.3 4.5 convolution_convert_fusion.4
  503.8 57.0 %reduce-scatter.23.cloned.1.call-done = f32[4,64,1280]{2,1,0:T(8,128)} async-done(((f32[4,256,1280]{2,1,0:T(8,128)}), f32[4,64,1280]{2,1,0:T(8,128)}) %reduce-scatter.23.cloned.1.call-update) | async-done | bytes 1310736 | tf_op jit(solution)/shard_map/reduce_scatter | solution.py:172
  563.2 40.1 %reduce-scatter.21.cloned.1.call-done = bf16[4,64,1280]{2,1,0:T(8,128)(2,1)} async-done(((bf16[4,256,1280]{2,1,0:T(8,128)(2,1)}), bf16[4,64,1280]{2,1,0:T(8,128)(2,1)}) %reduce-scatter.21.cloned.1.call-update) | async-done | bytes 655376 | tf_op jit(solution)/shard_map/reduce_scatter | solution.py:154
  608.3 39.7 %all-gather.14.cloned.1.call-done = bf16[4,256,1280]{2,1,0:T(8,128)(2,1)} async-done(((bf16[4,64,1280]{2,1,0:T(8,128)(2,1)}), bf16[4,256,1280]{2,1,0:T(8,128)(2,1)}) %all-gather.14.cloned.1.call-update) | async-done | bytes 2621456 | tf_op jit(solution)/shard_map/all_gather | solution.py:176
  648.0 3.9 convolution_convert_fusion.7
  651.9 174.2 %while.27 = (s32[]{:T(128)}, bf16[4,256,64]{1,2,0:T(8,128)(2,1)S(1)}, bf16[4,4096,64]{1,2,0:T(8,128)(2,1)S(1)}, bf16[4,4096,320]{1,2,0:T(8,128)(2,1)}, bf16[4,40...) while((s32[]{:T(128)}, ...), condition=%wide.region_17.18_spmd, body=%wide.region_15.17_spmd.sunk | while | flops 1772368896 | bytes 112507056 | solution.py:181
  661.1 3.7 constant_dynamic-update-slice_fusion.7
  664.8 5.0 fusion.142
  669.7 12.7 fusion.143
  682.5 13.0 convolution_convert_fusion.10
  704.5 3.9 constant_dynamic-update-slice_fusion.7
  708.4 5.0 fusion.142
  713.4 12.7 fusion.143
  726.1 13.0 convolution_convert_fusion.10
  748.2 3.7 constant_dynamic-update-slice_fusion.7
  751.9 5.0 fusion.142
  756.8 12.7 fusion.143
  769.6 13.0 convolution_convert_fusion.10
  791.6 3.7 constant_dynamic-update-slice_fusion.7
  795.4 5.0 fusion.142
  800.3 12.7 fusion.143
  813.1 13.0 convolution_convert_fusion.10
  827.8 4.5 fusion.30
  832.4 4.5 fusion.29
  837.0 10.8 fusion.38
  848.6 25.0 %fusion.47 = f32[4,4096,768]{2,1,0:T(8,128)} fusion(bf16[4,4096,320]{1,2,0:T(8,128)(2,1)} %get-tuple-element.112, bf16[768,320]{1,0:T(8,128)(2,1)S(1)} %copy-done.10), kind=kOutput, calls=%fused_computation.115 | convolution fusion | flops 8053063680 | bytes 61308928 | tf_op jit(solution)/shard_map/slv,cv->slc/dot_general | solution.py:198
  876.3 20.4 %fusion.31 = bf16[768,320]{1,0:T(8,128)(2,1)} fusion(bf16[4,4096,768]{2,1,0:T(8,128)(2,1)} %all-gather.8.cloned.1.call-done, bf16[4,4096,320]{1,2,0:T(8,128)(2,1)} %get-tuple-element.112), kind=kOutput, calls=%fused_computation.74 | convolution fusion | flops 8053309440 | bytes 36143104 | tf_op jit(solution)/shard_map/slc,slv->cv/dot_general | solution.py:194
  901.3 4.5 fusion.28
  906.1 25.7 %add_convert_fusion = bf16[4,4096,768]{2,1,0:T(8,128)(2,1)} fusion(f32[4,4096,768]{2,1,0:T(8,128)} %fusion.47, bf16[4,4096,64]{1,2,0:T(8,128)(2,1)S(1)} %get-tuple-element.111, bf16[768,64,1]{0,1,2:T(8,128)(2,1)S(1)} %copy-done.16), kind=kOutput, calls=%fused_computation.38 | convolution fusion | flops 1635778560 | bytes 77692928 | tf_op jit(solution)/shard_map/slq,cq->slc/dot_general | solution.py:197
  935.9 15.7 %reduce-scatter.41.cloned.1.call-done = bf16[96,64]{1,0:T(8,128)(2,1)} async-done(((bf16[768,64]{1,0:T(8,128)(2,1)}), bf16[96,64]{1,0:T(8,128)(2,1)}) %reduce-scatter.41.cloned.1.call-update) | async-done | bytes 12304
  953.0 29.3 %reduce-scatter.39.cloned.1.call-done = bf16[160,64]{1,0:T(8,128)(2,1)} async-done(((bf16[1280,64]{1,0:T(8,128)(2,1)}), bf16[160,64]{1,0:T(8,128)(2,1)}) %reduce-scatter.39.cloned.1.call-update) | async-done | bytes 20496
  983.8 30.2 %reduce-scatter.29.cloned.1.call-done = bf16[96,320]{1,0:T(8,128)(2,1)} async-done(((bf16[768,320]{1,0:T(8,128)(2,1)}), bf16[96,320]{1,0:T(8,128)(2,1)}) %reduce-scatter.29.cloned.1.call-update) | async-done | bytes 61456 | tf_op jit(solution)/shard_map/reduce_scatter | solution.py:221
  1015.6 29.3 %reduce-scatter.37.cloned.1.call-done = bf16[160,64]{1,0:T(8,128)(2,1)} async-done(((bf16[1280,64]{1,0:T(8,128)(2,1)}), bf16[160,64]{1,0:T(8,128)(2,1)}) %reduce-scatter.37.cloned.1.call-update) | async-done | bytes 20496
  1046.3 31.4 %reduce-scatter.31.cloned.1.call-done = bf16[320,160]{0,1:T(8,128)(2,1)} async-done(((bf16[320,1280]{0,1:T(8,128)(2,1)}), bf16[320,160]{0,1:T(8,128)(2,1)}) %reduce-scatter.31.cloned.1.call-update) | async-done | bytes 102416 | tf_op jit(solution)/shard_map/reduce_scatter | solution.py:227
  1079.3 222.0 %reduce-scatter.25.cloned.1.call-done = bf16[4,1024,768]{2,1,0:T(8,128)(2,1)} async-done(((bf16[4,4096,768]{2,1,0:T(8,128)(2,1)}), bf16[4,1024,768]{2,1,0:T(8,128)(2,1)}) %reduce-scatter.25.cloned.1.call-update) | async-done | bytes 6291472 | tf_op jit(solution)/shard_map/reduce_scatter | solution.py:205
  1301.3 7.7 convert_reduce_fusion
  1309.1 9.1 fusion.25
  1318.3 40.9 %all-reduce = (f32[768]{0:T(1024)}, f32[768]{0:T(1024)}, f32[1280]{0:T(1024)}, f32[1280]{0:T(1024)}, f32[1280]{0:T(1024)}, /*index=5*/f32[1280]{0:T(1024)}, f32[1280]{0:T(1024)}, f32[1280]{0:T(1024)}) all-reduce(f32[768]{0:T(1024)S(1)} %get-tuple-element.114, ...), channel_id=1, replica_groups=mesh['dp'=8,'tensor'=4] {'dp','tensor'}, use_global_device_ids=true, to_apply=%region_28.29 | all-reduce | flops 9216 | bytes 73728 | tf_op jit(solution)/shard_map/psum | solution.py:250
  1359.2 12.7 fusion.26
  (269 shorter events, 117.7 us)
Async XLA Ops:
  7.2 247.6 %all-gather.8.cloned.1.call-start = ((), (), s32[]{:S(2)}) async-start(), calls=%async_computation.12 | async-start | bytes 31457280 | tf_op jit(solution)/shard_map/all_gather | solution.py:125
  7.2 4.6 copy-start
  11.8 2.5 copy-start.18
  11.8 3.1 copy-start.31
  11.8 3.1 copy-start.46
  19.3 16.7 %copy-start.36 = (bf16[64,160]{1,0:T(8,128)(2,1)S(1)}, bf16[64,160]{1,0:T(8,128)(2,1)}, u32[]{:S(2)}) copy-start(bf16[64,160]{1,0:T(8,128)(2,1)} %param.24) | copy-start | bytes 61444
  19.3 31.2 %copy-start.37 = (bf16[160,64]{0,1:T(8,128)(2,1)S(1)}, bf16[160,64]{0,1:T(8,128)(2,1)}, u32[]{:S(2)}) copy-start(bf16[160,64]{0,1:T(8,128)(2,1)} %param.29) | copy-start | bytes 61444
  19.3 385.8 %reduce-scatter.19.cloned.1.call-start = ((), (), s32[]{:S(2)}) async-start(), calls=%async_computation.13 | async-start | bytes 6553600 | tf_op jit(solution)/shard_map/reduce_scatter | solution.py:136
  35.7 29.9 %copy-start.24 = (f32[1280]{0:T(1024)S(1)}, f32[1280]{0:T(1024)}, u32[]{:S(2)}) copy-start(f32[1280]{0:T(1024)} %param.27) | copy-start | bytes 15364
  35.7 29.9 %copy-start.41 = (f32[1280]{0:T(1024)S(1)}, f32[1280]{0:T(1024)}, u32[]{:S(2)}) copy-start(f32[1280]{0:T(1024)} %param.28) | copy-start | bytes 15364
  35.9 218.9 %copy-start.15 = (bf16[768,64,1]{0,1,2:T(8,128)(2,1)}, bf16[768,64,1]{0,1,2:T(8,128)(2,1)S(1)}, u32[]{:S(2)}) copy-start(bf16[768,64,1]{0,1,2:T(8,128)(2,1)S(1)} %reshape.241) | copy-start | bytes 294916
  50.3 33.2 %copy-start.30 = (bf16[96,320]{1,0:T(8,128)(2,1)S(1)}, bf16[96,320]{1,0:T(8,128)(2,1)}, u32[]{:S(2)}) copy-start(bf16[96,320]{1,0:T(8,128)(2,1)} %param.31) | copy-start | bytes 184324
  64.8 35.2 %copy-start.26 = (bf16[320,160]{0,1:T(8,128)(2,1)S(1)}, bf16[320,160]{0,1:T(8,128)(2,1)}, u32[]{:S(2)}) copy-start(bf16[320,160]{0,1:T(8,128)(2,1)} %param.32) | copy-start | bytes 307204
  65.2 51.9 %copy-start.11 = (bf16[1280,64]{0,1:T(8,128)(2,1)}, bf16[1280,64]{0,1:T(8,128)(2,1)S(1)}, u32[]{:S(2)}) copy-start(bf16[1280,64]{0,1:T(8,128)(2,1)S(1)} %reshape.238) | copy-start | bytes 491524
  65.3 51.7 %copy-start.39 = (f32[64]{0:T(128)}, f32[64]{0:T(128)S(1)}, u32[]{:S(2)}) copy-start(f32[64]{0:T(128)S(1)} %broadcast_multiply_fusion.2) | copy-start | bytes 772
  65.5 51.5 %copy-start.48 = (f32[64]{0:T(128)}, f32[64]{0:T(128)S(1)}, u32[]{:S(2)}) copy-start(f32[64]{0:T(128)S(1)} %multiply_reduce_fusion.3) | copy-start | bytes 772
  65.6 51.5 %copy-start.44 = (f32[64]{0:T(128)}, f32[64]{0:T(128)S(1)}, u32[]{:S(2)}) copy-start(f32[64]{0:T(128)S(1)} %fusion.60) | copy-start | bytes 772
  83.5 16.1 %copy-start.5 = (bf16[256,1280]{1,0:T(8,128)(2,1)}, bf16[256,1280]{1,0:T(8,128)(2,1)S(1)}, u32[]{:S(2)}) copy-start(bf16[256,1280]{1,0:T(8,128)(2,1)S(1)} %all_gather.40) | copy-start | bytes 1966084
  117.1 221.0 %copy-start.7 = (bf16[320,1280]{0,1:T(8,128)(2,1)}, bf16[320,1280]{0,1:T(8,128)(2,1)S(1)}, u32[]{:S(2)}) copy-start(bf16[320,1280]{0,1:T(8,128)(2,1)S(1)} %all_gather.42) | copy-start | bytes 2457604
  254.8 15.8 %copy-start.9 = (bf16[768,320]{1,0:T(8,128)(2,1)S(1)}, bf16[768,320]{1,0:T(8,128)(2,1)}, u32[]{:S(2)}) copy-start(bf16[768,320]{1,0:T(8,128)(2,1)} %all_gather.38) | copy-start | bytes 1474564
  270.7 17.0 %copy-start.50 = (s32[4]{0:T(128)S(1)}, s32[4]{0:T(128)}, u32[]{:S(2)}) copy-start(s32[4]{0:T(128)} %param.23) | copy-start | bytes 52
  338.1 5.4 copy-start.4
  343.5 63.6 %copy-start.29 = (f32[1280]{0:T(1024)S(1)}, f32[1280]{0:T(1024)}, u32[]{:S(2)}) copy-start(f32[1280]{0:T(1024)} %param.33) | copy-start | bytes 15364
  343.5 63.6 %copy-start.42 = (f32[1280]{0:T(1024)S(1)}, f32[1280]{0:T(1024)}, u32[]{:S(2)}) copy-start(f32[1280]{0:T(1024)} %param.34) | copy-start | bytes 15364
  343.5 104.6 %all-gather.10.cloned.1.call-start = ((), (), s32[]{:S(2)}) async-start(), calls=%async_computation.14 | async-start | bytes 3276800 | tf_op jit(solution)/shard_map/all_gather | solution.py:141
  405.1 1.7 copy-start.3
  406.8 1.6 copy-start.6
  408.3 1.9 copy-start.27
  408.3 19.0 %copy-start.28 = (bf16[320,160]{0,1:T(8,128)(2,1)S(1)}, bf16[320,160]{0,1:T(8,128)(2,1)}, u32[]{:S(2)}) copy-start(bf16[320,160]{0,1:T(8,128)(2,1)} %param.37) | copy-start | bytes 307204
  408.3 81.2 %all-gather.12.cloned.1.call-start = ((), (), s32[]{:S(2)}) async-start(), calls=%async_computation.16 | async-start | bytes 3276800 | tf_op jit(solution)/shard_map/all_gather | solution.py:142
  409.3 151.4 %reduce-scatter.23.cloned.1.call-start = ((), (), s32[]{:S(2)}) async-start(), calls=%async_computation.17 | async-start | bytes 6553600 | tf_op jit(solution)/shard_map/reduce_scatter | solution.py:172
  489.5 5.8 copy-start.8
  499.2 104.0 %reduce-scatter.21.cloned.1.call-start = ((), (), s32[]{:S(2)}) async-start(), calls=%async_computation.15 | async-start | bytes 3276800 | tf_op jit(solution)/shard_map/reduce_scatter | solution.py:154
  503.8 99.5 %copy-start.43 = (f32[1280]{0:T(1024)S(1)}, f32[1280]{0:T(1024)}, u32[]{:S(2)}) copy-start(f32[1280]{0:T(1024)} %param.38) | copy-start | bytes 15364
  503.8 144.2 %all-gather.14.cloned.1.call-start = ((), (), s32[]{:S(2)}) async-start(), calls=%async_computation.18 | async-start | bytes 3276800 | tf_op jit(solution)/shard_map/all_gather | solution.py:176
  608.2 288.6 %reduce-scatter.27.cloned.1.call-start = ((), (), s32[]{:S(2)}) async-start(), calls=%async_computation.20 | async-start | bytes 819200 | tf_op jit(solution)/shard_map/reduce_scatter | solution.py:202
  651.9 174.3 %copy-start.12 = (bf16[1280,64]{0,1:T(8,128)(2,1)S(1)}, bf16[1280,64]{0,1:T(8,128)(2,1)}, u32[]{:S(2)}) copy-start(bf16[1280,64]{0,1:T(8,128)(2,1)} %copy-done.11) | copy-start | bytes 491524
  657.9 3.2 copy-start.1
  701.3 3.2 copy-start.1
  745.0 3.2 copy-start.1
  788.4 3.2 copy-start.1
  827.4 105.3 %reduce-scatter.35.cloned.1.call-start = ((), (), s32[]{:S(2)}) async-start(), calls=%async_computation.24 | async-start | bytes 1105920 | tf_op jit(solution)/shard_map/reduce_scatter | solution.py:230
  832.4 101.9 %reduce-scatter.33.cloned.1.call-start = ((), (), s32[]{:S(2)}) async-start(), calls=%async_computation.23 | async-start | bytes 1105920 | tf_op jit(solution)/shard_map/reduce_scatter | solution.py:224
  836.9 114.7 %reduce-scatter.41.cloned.1.call-start = ((), (), s32[]{:S(2)}) async-start(), calls=%async_computation.27 | async-start | bytes 221184
  837.0 11.6 copy-start.10
  873.7 108.6 %reduce-scatter.39.cloned.1.call-start = ((), (), s32[]{:S(2)}) async-start(), calls=%async_computation.26 | async-start | bytes 368640
  876.0 20.8 %copy-start.25 = (f32[1280]{0:T(1024)S(1)}, f32[1280]{0:T(1024)}, u32[]{:S(2)}) copy-start(f32[1280]{0:T(1024)} %param.27) | copy-start | bytes 15364
  876.0 20.8 %copy-start.40 = (f32[64]{0:T(128)S(1)}, f32[64]{0:T(128)}, u32[]{:S(2)}) copy-start(f32[64]{0:T(128)} %copy-done.39) | copy-start | bytes 772
  876.0 21.9 %copy-start.49 = (f32[64]{0:T(128)S(1)}, f32[64]{0:T(128)}, u32[]{:S(2)}) copy-start(f32[64]{0:T(128)} %copy-done.48) | copy-start | bytes 772
  876.0 21.9 %copy-start.45 = (f32[64]{0:T(128)S(1)}, f32[64]{0:T(128)}, u32[]{:S(2)}) copy-start(f32[64]{0:T(128)} %copy-done.44) | copy-start | bytes 772
  876.1 23.2 %copy-start.13 = (f32[64,1280]{1,0:T(8,128)S(1)}, f32[64,1280]{1,0:T(8,128)}, u32[]{:S(2)}) copy-start(f32[64,1280]{1,0:T(8,128)} %get-tuple-element.121) | copy-start | bytes 983044
  876.1 138.0 %reduce-scatter.29.cloned.1.call-start = ((), (), s32[]{:S(2)}) async-start(), calls=%async_computation.21 | async-start | bytes 663552 | tf_op jit(solution)/shard_map/reduce_scatter | solution.py:221
  896.7 148.1 %reduce-scatter.37.cloned.1.call-start = ((), (), s32[]{:S(2)}) async-start(), calls=%async_computation.25 | async-start | bytes 368640
  901.3 4.9 copy-start.16
  901.3 176.4 %reduce-scatter.31.cloned.1.call-start = ((), (), s32[]{:S(2)}) async-start(), calls=%async_computation.22 | async-start | bytes 1105920 | tf_op jit(solution)/shard_map/reduce_scatter | solution.py:227
  905.9 395.4 %reduce-scatter.25.cloned.1.call-start = ((), (), s32[]{:S(2)}) async-start(), calls=%async_computation.19 | async-start | bytes 31457280 | tf_op jit(solution)/shard_map/reduce_scatter | solution.py:205
  931.9 369.4 %copy-start.19 = (f32[4,1024]{1,0:T(4,128)S(1)}, f32[4,1024]{1,0:T(4,128)}, u32[]{:S(2)}) copy-start(f32[4,1024]{1,0:T(4,128)} %copy-done.18) | copy-start | bytes 49156
  931.9 369.4 %copy-start.32 = (f32[768]{0:T(1024)S(1)}, f32[768]{0:T(1024)}, u32[]{:S(2)}) copy-start(f32[768]{0:T(1024)} %param.25) | copy-start | bytes 9220
  1079.3 229.7 %copy-start.23 = (f32[4,1024]{1,0:T(4,128)S(1)}, f32[4,1024]{1,0:T(4,128)}, u32[]{:S(2)}) copy-start(f32[4,1024]{1,0:T(4,128)} %copy-done.22) | copy-start | bytes 49156
  1079.3 229.8 %copy-start.21 = (f32[4,1024]{1,0:T(4,128)S(1)}, f32[4,1024]{1,0:T(4,128)}, u32[]{:S(2)}) copy-start(f32[4,1024]{1,0:T(4,128)} %copy-done.20) | copy-start | bytes 49156
  1301.3 7.8 copy-start.2
  1309.1 9.2 copy-start.33
  1309.1 9.2 copy-start.34
  1309.1 9.2 copy-start.35
  (6 other events, 4.5 us)
Sparse Core Ops, SparseCore 0:
  19.4 235.3 all-gather.7
  343.6 61.4 reduce-scatter.18
  408.5 39.6 all-gather.9
  449.8 39.6 all-gather.11
  499.3 61.4 reduce-scatter.22
  563.6 39.5 reduce-scatter.20
  608.3 39.6 all-gather.13
  827.5 25.3 reduce-scatter.26
  855.4 32.2 reduce-scatter.34
  889.8 30.2 reduce-scatter.32
  923.0 28.5 reduce-scatter.40
  953.7 28.5 reduce-scatter.38
  984.7 29.2 reduce-scatter.28
  1016.2 28.5 reduce-scatter.36
  1047.5 30.1 reduce-scatter.30
  1081.0 220.2 reduce-scatter.24
where the time goes:
time: 1390 us; the launch traced here: 1380 us
  waiting for transfers between devices  730 us (53%)
  matrix products  319 us (23%)
  blocking collectives  171 us (12%)
  other arithmetic  83.7 us (6%)
  local copies, waits for them, and re-layouts  58.1 us (4%)
  between operations  14.9 us (1%)
    reduce_scatter x1, waiting for transfers between devices, on_device(): lax.psum_scatter(byte_term.astype(jnp.bfloat16), 'tensor', scatter_dimens...  222 us
    all_gather x1, waiting for transfers between devices, on_device(): lax.all_gather(byte_norm, 'tensor', axis=1, tiled=True)  138 us
    unnamed x19, waiting for transfers between devices  74.4 us
    reduce_scatter x1, waiting for transfers between devices, on_device(): lax.psum_scatter(attn_term, 'tensor', scatter_dimension=1, tiled=True)  61.5 us
    reduce_scatter x1, waiting for transfers between devices, on_device(): lax.psum_scatter(hidden_term, 'tensor', scatter_dimension=1, tiled=True)  57 us
    dot_general x4, matrix products, score_backward(): jnp.einsum('hnl,nhd->lhd', grad_scores, query_heads, preferred_element_ty...  51.9 us
    dot_general x4, matrix products, score_backward(): jnp.einsum('hnl,lhd->nhd', grad_scores, key_heads, preferred_element_type...  50.9 us
    psum x1, blocking collectives, on_device(): lax.psum((grad_g_in, grad_b_in, grad_g_lat, grad_b_lat, grad_g_mlp, grad_...  40.9 us
  transfers between devices with their start and end apart: 16, of which 13 were waited for; matrix products, arithmetic and copies ran while one was open for 10% of the time, Pallas kernels for 0%

commit v1 on v0

--- a/solution.py
+++ b/solution.py
@@ -7,6 +7,28 @@
 HQ = 32
 HV = 160
 NEGATIVE = -1e30
+
+
+def in_order(blocks, dim):
+    lengths = list(blocks.shape[1:])
+    lengths[dim] *= blocks.shape[0]
+    return jnp.moveaxis(blocks, 0, dim).reshape(lengths)
+
+
+def gather_around(shard, axis, dim):
+    devices = lax.axis_size(axis)
+    pairs = [(i, (i + 1) % devices) for i in range(devices)]
+    back = [(b, a) for a, b in pairs]
+    lower, upper = ([], [])
+    for step in range(devices - 1):
+        if step % 2 == 0:
+            lower.append(lax.ppermute(lower[-1] if lower else shard, axis, pairs))
+        else:
+            upper.append(lax.ppermute(upper[-1] if upper else shard, axis, back))
+    pieces = jnp.stack([*lower[::-1], shard, *upper])
+    shift = lax.axis_index(axis) - len(lower)
+    pieces = pieces[(jnp.arange(devices) - shift) % devices]
+    return in_order(pieces, dim)
 
 
 def normalize(values, gain, shift):
@@ -122,7 +144,7 @@
     byte_norm = normalize(byte_float, g_in, b_in).astype(jnp.bfloat16)
     latent_all, byte_all = (
         lax.all_gather(latent_norm, "tensor", axis=0, tiled=True),
-        lax.all_gather(byte_norm, "tensor", axis=1, tiled=True),
+        gather_around(byte_norm, "tensor", 1),
     )
     keys = jnp.einsum("slc,cq->slq", byte_all, full_key, preferred_element_type=jnp.float32).astype(
         jnp.bfloat16

time: 1390 us -> 1710 us (1.23)
  blocking collectives: 171 us -> 381 us
  local copies, waits for them, and re-layouts: 58.1 us -> 121 us
  other arithmetic: 83.7 us -> 126 us
    all_gather x1, blocking collectives: 17.8 us -> 229 us  [on_device(): lax.all_gather(latent_norm, 'tensor', axis=0, tiled=True)]
    all_gather x1 -> x0, waiting for transfers between devices: 138 us -> none  [on_device(): lax.all_gather(byte_norm, 'tensor', axis=1, tiled=True)]
    ppermute x0 -> x3, waiting for transfers between devices: none -> 137 us  [the longest x2 137 us: gather_around(): lower.append(lax.ppermute(lower[-1] if lower else shard, axis, pairs))]
    gather x0 -> x5, local copies, waits for them, and re-layouts: none -> 43.5 us  [gather_around(): pieces = pieces[(jnp.arange(devices) - shift) % devices]]
    another operation x0 -> x2, other arithmetic: none -> 23.6 us  [gather_around(): pieces = jnp.stack([*lower[::-1], shard, *upper])]
    transpose x0 -> x1, local copies, waits for them, and re-layouts: none -> 20.8 us  [in_order(): return jnp.moveaxis(blocks, 0, dim).reshape(lengths)]
    transpose x0 -> x1, other arithmetic: none -> 17.7 us  [in_order(): return jnp.moveaxis(blocks, 0, dim).reshape(lengths)]
    unnamed x19 -> x18, waiting for transfers between devices: 74.4 us -> 75.5 us
  transfers between devices with their start and end apart: 16 -> 18, of which waited for: 13 -> 13; matrix products, arithmetic and copies ran while one was open for 10% -> 8% of each run, Pallas kernels for 0% -> 0%
where the time goes in v1:
time: 1710 us; the launch traced here: 1700 us
  waiting for transfers between devices  731 us (43%)
  blocking collectives  381 us (22%)
  matrix products  319 us (19%)
  other arithmetic  126 us (7%)
  local copies, waits for them, and re-layouts  121 us (7%)
    all_gather x1, blocking collectives, on_device(): lax.all_gather(latent_norm, 'tensor', axis=0, tiled=True)  229 us
    reduce_scatter x1, waiting for transfers between devices, on_device(): lax.psum_scatter(byte_term.astype(jnp.bfloat16), 'tensor', scatter_dimens...  222 us
    ppermute x2, waiting for transfers between devices, gather_around(): lower.append(lax.ppermute(lower[-1] if lower else shard, axis, pairs))  137 us
    unnamed x18, waiting for transfers between devices  75.5 us
    reduce_scatter x1, waiting for transfers between devices, on_device(): lax.psum_scatter(attn_term, 'tensor', scatter_dimension=1, tiled=True)  62.3 us
    reduce_scatter x1, waiting for transfers between devices, on_device(): lax.psum_scatter(hidden_term, 'tensor', scatter_dimension=1, tiled=True)  57 us
    dot_general x4, matrix products, score_backward(): jnp.einsum('hnl,nhd->lhd', grad_scores, query_heads, preferred_element_ty...  51.9 us
    dot_general x4, matrix products, score_backward(): jnp.einsum('hnl,lhd->nhd', grad_scores, key_heads, preferred_element_type...  50.9 us
  transfers between devices with their start and end apart: 18, of which 13 were waited for; matrix products, arithmetic and copies ran while one was open for 8% of the time, Pallas kernels for 0%

profile of v1, /device:TPU:0, one launch (start us, length us, event | category | flops | bytes accessed | tf_op | source)
XLA Modules:
  0.0 1699.7 jit_solution(10432254371810510722)
XLA Ops:
  13.9 4.3 fusion.22
  22.1 136.6 %collective-permute-done = bf16[4,1024,768]{2,1,0:T(8,128)(2,1)} collective-permute-done((bf16[4,1024,768]{2,1,0:T(8,128)(2,1)}, bf16[4,1024,768]{2,1,0:T(8,128)(2,1)}, u32[]{:S(2)}, u32[]{:S(2)}) %collective-permute-start) | collective-permute-done | bytes 6291488 | tf_op jit(solution)/shard_map/ppermute | solution.py:25
  159.8 14.2 all-gather.1
  174.4 14.2 all-gather
  189.0 14.2 all-gather.2
  204.2 229.4 %all_gather.36 = bf16[256,1280]{1,0:T(8,128)(2,1)S(1)} all-gather(bf16[64,1280]{1,0:T(8,128)(2,1)S(1)} %add_convert_fusion.4), channel_id=1, replica_groups=mesh['dp'=8,'tensor'=4] {'tensor'}, dimensions={0}, use_global_device_ids=true | all-gather | bytes 819200 | tf_op jit(solution)/shard_map/all_gather | solution.py:146
  433.5 15.3 all_gather.34
  449.2 17.9 %all_gather.38 = bf16[320,1280]{0,1:T(8,128)(2,1)} all-gather(bf16[320,160]{0,1:T(8,128)(2,1)S(1)} %copy-done.28), channel_id=1, replica_groups=mesh['dp'=8,'tensor'=4] {'dp'}, dimensions={1}, use_global_device_ids=true | all-gather | bytes 921600 | tf_op jit(solution)/shard_map/all_gather | solution.py:136
  467.1 4.9 fusion.114
  472.0 18.7 %pad_maximum_fusion = bf16[4,4,1024,768]{3,2,1,0:T(8,128)(2,1)} fusion(bf16[1,4,1024,768]{3,2,1,0:T(8,128)(2,1)} %bitcast.27, bf16[1,4,1024,768]{3,2,1,0:T(8,128)(2,1)S(1)} %fusion.114, bf16[1,4,1024,768]{3,2,1,0:T(8,128)(2,1)} %bitcast.25, bf16[1,4,1024,768]{3,2,1,0:T(8,128)(2,1)} %bitcast.24), kind=kLoop, calls=%fused_computation.43 | loop fusion | flops 37748736 | bytes 50331648 | tf_op jit(solution)/shard_map/stack | solution.py:28
  490.7 18.1 %fusion.68 = (bf16[4,4,256,768]{3,2,1,0:T(8,128)(2,1)}, bf16[4,4,256,768]{3,2,1,0:T(8,128)(2,1)}, bf16[4,4,256,768]{3,2,1,0:T(8,128)(2,1)}, bf16[4,4,256,768]{3,2,1,0:T(8,128)(2,1)}) fusion(bf16[4,4,1024,768]{3,2,1,0:T(8,128)(2,1)} %pad_maximum_fusion), kind=kLoop, calls=%fused_computation.166 | loop fusion | bytes 50331648 | tf_op jit(solution)/shard_map/gather | solution.py:30
  508.8 6.3 gather_fusion
  515.1 6.4 gather_fusion.2
  521.5 6.3 gather_fusion.1
  527.8 6.4 gather_fusion.3
  534.2 17.7 %maximum_bitcast_fusion = bf16[4,4,1024,768]{3,2,0,1:T(8,128)(2,1)} fusion(bf16[4,4,256,768]{3,2,1,0:T(8,128)(2,1)} %gather_fusion.3, bf16[4,4,256,768]{3,2,1,0:T(8,128)(2,1)} %gather_fusion.2, bf16[4,4,256,768]{3,2,1,0:T(8,128)(2,1)} %gather_fusion.1, bf16[4,4,256,768]{3,2,1,0:T(8,128)(2,1)} %gather_fusion), kind=kLoop, calls=%fused_computation.44 | loop fusion | flops 100663296 | bytes 50331648 | tf_op jit(solution)/shard_map/transpose | solution.py:15
  551.9 20.8 %copy.63 = bf16[4,4,1024,768]{3,2,1,0:T(8,128)(2,1)} copy(bf16[4,4,1024,768]{3,2,0,1:T(8,128)(2,1)} %maximum_bitcast_fusion) | data formatting | bytes 50331648 | tf_op jit(solution)/shard_map/transpose | solution.py:15
  572.7 15.8 convolution_convert_fusion.3
  588.5 17.0 %convolution_convert_fusion.2 = bf16[4,4096,320]{1,2,0:T(8,128)(2,1)} fusion(bf16[4,4096,768]{2,1,0:T(8,128)(2,1)} %bitcast.256, bf16[768,320]{1,0:T(8,128)(2,1)S(1)} %all_gather.34), kind=kOutput, calls=%fused_computation.62 | convolution fusion | flops 8058306560 | bytes 36143104 | tf_op jit(solution)/shard_map/slc,cv->slv/dot_general | solution.py:152
  605.5 50.5 %while.26 = (s32[]{:T(128)}, bf16[4,256,320]{1,2,0:T(8,128)(2,1)}, f32[4,2,256]{2,1,0:T(2,128)S(1)}, bf16[4,4096,320]{1,2,0:T(8,128)(2,1)}, s32[4]{0:T(128)S(1)}...) while((s32[]{:T(128)}, bf16[4,256,320]{1,2,0:T(8,128)(2,1)}, ...), condition=%wide.region_7.8_spmd, body=%wide.region_4.7_spmd.sunk | while | flops 830557696 | bytes 35160188 | solution.py:156
  656.0 5.4 fusion.45
  661.6 62.3 %reduce-scatter.19.cloned.1.call-done = f32[4,64,1280]{2,1,0:T(8,128)} async-done(((f32[4,256,1280]{2,1,0:T(8,128)}), f32[4,64,1280]{2,1,0:T(8,128)}) %reduce-scatter.19.cloned.1.call-update) | async-done | bytes 1310736 | tf_op jit(solution)/shard_map/reduce_scatter | solution.py:158
  730.3 17.2 %all_gather.40 = bf16[1280,320]{1,0:T(8,128)(2,1)} all-gather(bf16[160,320]{1,0:T(8,128)(2,1)S(1)} %copy-done.29), channel_id=1, replica_groups=mesh['dp'=8,'tensor'=4] {'dp'}, dimensions={0}, use_global_device_ids=true | all-gather | bytes 921600 | tf_op jit(solution)/shard_map/all_gather | solution.py:135
  747.4 17.6 %all_gather.41 = bf16[320,1280]{0,1:T(8,128)(2,1)} all-gather(bf16[320,160]{0,1:T(8,128)(2,1)S(1)} %copy-done.30), channel_id=1, replica_groups=mesh['dp'=8,'tensor'=4] {'dp'}, dimensions={1}, use_global_device_ids=true | all-gather | bytes 921600 | tf_op jit(solution)/shard_map/all_gather | solution.py:137
  772.7 4.1 multiply_convert_fusion
  776.8 33.0 %all-gather.9.cloned.1.call-done = bf16[4,256,1280]{2,1,0:T(8,128)(2,1)} async-done(((bf16[4,64,1280]{2,1,0:T(8,128)(2,1)}), bf16[4,256,1280]{2,1,0:T(8,128)(2,1)}) %all-gather.9.cloned.1.call-update) | async-done | bytes 2621456 | tf_op jit(solution)/shard_map/all_gather | solution.py:164
  809.7 5.0 convert_reduce_fusion.2
  815.6 3.9 fusion.41
  819.5 4.5 convolution_convert_fusion.4
  824.1 57.0 %reduce-scatter.23.cloned.1.call-done = f32[4,64,1280]{2,1,0:T(8,128)} async-done(((f32[4,256,1280]{2,1,0:T(8,128)}), f32[4,64,1280]{2,1,0:T(8,128)}) %reduce-scatter.23.cloned.1.call-update) | async-done | bytes 1310736 | tf_op jit(solution)/shard_map/reduce_scatter | solution.py:194
  883.4 40.0 %reduce-scatter.21.cloned.1.call-done = bf16[4,64,1280]{2,1,0:T(8,128)(2,1)} async-done(((bf16[4,256,1280]{2,1,0:T(8,128)(2,1)}), bf16[4,64,1280]{2,1,0:T(8,128)(2,1)}) %reduce-scatter.21.cloned.1.call-update) | async-done | bytes 655376 | tf_op jit(solution)/shard_map/reduce_scatter | solution.py:176
  928.6 39.7 %all-gather.11.cloned.1.call-done = bf16[4,256,1280]{2,1,0:T(8,128)(2,1)} async-done(((bf16[4,64,1280]{2,1,0:T(8,128)(2,1)}), bf16[4,256,1280]{2,1,0:T(8,128)(2,1)}) %all-gather.11.cloned.1.call-update) | async-done | bytes 2621456 | tf_op jit(solution)/shard_map/all_gather | solution.py:198
  968.3 3.9 convolution_convert_fusion.7
  972.2 174.4 %while.27 = (s32[]{:T(128)}, bf16[4,256,64]{1,2,0:T(8,128)(2,1)S(1)}, bf16[4,4096,64]{1,2,0:T(8,128)(2,1)S(1)}, bf16[4,4096,320]{1,2,0:T(8,128)(2,1)}, bf16[4,40...) while((s32[]{:T(128)}, ...), condition=%wide.region_17.18_spmd, body=%wide.region_15.17_spmd.sunk | while | flops 1772368896 | bytes 112507056 | solution.py:203
  985.3 5.0 fusion.146
  990.3 12.7 fusion.147
  1003.0 13.0 convolution_convert_fusion.10
  1025.1 3.9 constant_dynamic-update-slice_fusion.7
  1028.9 5.0 fusion.146
  1033.9 12.7 fusion.147
  1046.6 13.0 convolution_convert_fusion.10
  1072.4 5.0 fusion.146
  1077.4 12.7 fusion.147
  1090.1 13.0 convolution_convert_fusion.10
  1115.9 5.0 fusion.146
  1120.9 12.7 fusion.147
  1133.6 13.0 convolution_convert_fusion.10
  1148.1 4.5 fusion.30
  1152.7 4.4 fusion.29
  1157.2 10.8 fusion.38
  1168.8 25.0 %fusion.47 = f32[4,4096,768]{2,1,0:T(8,128)} fusion(bf16[4,4096,320]{1,2,0:T(8,128)(2,1)} %get-tuple-element.112, bf16[768,320]{1,0:T(8,128)(2,1)S(1)} %copy-done.12), kind=kOutput, calls=%fused_computation.121 | convolution fusion | flops 8053063680 | bytes 61308928 | tf_op jit(solution)/shard_map/slv,cv->slc/dot_general | solution.py:220
  1196.5 20.4 %fusion.31 = bf16[768,320]{1,0:T(8,128)(2,1)} fusion(bf16[4,4096,768]{2,1,0:T(8,128)(2,1)} %bitcast.258, bf16[4,4096,320]{1,2,0:T(8,128)(2,1)} %get-tuple-element.112), kind=kOutput, calls=%fused_computation.80 | convolution fusion | flops 8053309440 | bytes 36143104 | tf_op jit(solution)/shard_map/slc,slv->cv/dot_general | solution.py:216
  1221.6 4.5 fusion.28
  1226.4 25.7 %add_convert_fusion = bf16[4,4096,768]{2,1,0:T(8,128)(2,1)} fusion(f32[4,4096,768]{2,1,0:T(8,128)} %fusion.47, bf16[4,4096,64]{1,2,0:T(8,128)(2,1)S(1)} %get-tuple-element.111, bf16[768,64,1]{0,1,2:T(8,128)(2,1)S(1)} %copy-done.18), kind=kOutput, calls=%fused_computation.42 | convolution fusion | flops 1635778560 | bytes 77692928 | tf_op jit(solution)/shard_map/slq,cq->slc/dot_general | solution.py:219
  1256.2 16.2 reduce-scatter.41.cloned.1.call-done
  1273.8 29.5 %reduce-scatter.39.cloned.1.call-done = bf16[160,64]{1,0:T(8,128)(2,1)} async-done(((bf16[1280,64]{1,0:T(8,128)(2,1)}), bf16[160,64]{1,0:T(8,128)(2,1)}) %reduce-scatter.39.cloned.1.call-update) | async-done | bytes 20496
  1304.8 30.1 %reduce-scatter.29.cloned.1.call-done = bf16[96,320]{1,0:T(8,128)(2,1)} async-done(((bf16[768,320]{1,0:T(8,128)(2,1)}), bf16[96,320]{1,0:T(8,128)(2,1)}) %reduce-scatter.29.cloned.1.call-update) | async-done | bytes 61456 | tf_op jit(solution)/shard_map/reduce_scatter | solution.py:243
  1336.4 29.5 %reduce-scatter.37.cloned.1.call-done = bf16[160,64]{1,0:T(8,128)(2,1)} async-done(((bf16[1280,64]{1,0:T(8,128)(2,1)}), bf16[160,64]{1,0:T(8,128)(2,1)}) %reduce-scatter.37.cloned.1.call-update) | async-done | bytes 20496
  1367.5 31.3 %reduce-scatter.31.cloned.1.call-done = bf16[320,160]{0,1:T(8,128)(2,1)} async-done(((bf16[320,1280]{0,1:T(8,128)(2,1)}), bf16[320,160]{0,1:T(8,128)(2,1)}) %reduce-scatter.31.cloned.1.call-update) | async-done | bytes 102416 | tf_op jit(solution)/shard_map/reduce_scatter | solution.py:249
  1400.4 221.9 %reduce-scatter.25.cloned.1.call-done = bf16[4,1024,768]{2,1,0:T(8,128)(2,1)} async-done(((bf16[4,4096,768]{2,1,0:T(8,128)(2,1)}), bf16[4,1024,768]{2,1,0:T(8,128)(2,1)}) %reduce-scatter.25.cloned.1.call-update) | async-done | bytes 6291472 | tf_op jit(solution)/shard_map/reduce_scatter | solution.py:227
  1622.3 7.7 convert_reduce_fusion
  1630.2 9.1 fusion.25
  1639.3 40.9 %all-reduce = (f32[768]{0:T(1024)}, f32[768]{0:T(1024)}, f32[1280]{0:T(1024)}, f32[1280]{0:T(1024)}, f32[1280]{0:T(1024)}, /*index=5*/f32[1280]{0:T(1024)}, f32[1280]{0:T(1024)}, f32[1280]{0:T(1024)}) all-reduce(f32[768]{0:T(1024)S(1)} %get-tuple-element.114, ...), channel_id=1, replica_groups=mesh['dp'=8,'tensor'=4] {'dp','tensor'}, use_global_device_ids=true, to_apply=%region_28.29 | all-reduce | flops 9216 | bytes 73728 | tf_op jit(solution)/shard_map/psum | solution.py:272
  1680.2 12.7 fusion.26
  (287 shorter events, 154.8 us)
Async XLA Ops:
  7.2 716.7 %reduce-scatter.19.cloned.1.call-start = ((), (), s32[]{:S(2)}) async-start(), calls=%async_computation.12 | async-start | bytes 6553600 | tf_op jit(solution)/shard_map/reduce_scatter | solution.py:158
  7.2 4.6 copy-start
  11.8 455.2 %copy-start.19 = (f32[4,1024]{1,0:T(4,128)}, f32[4,1024]{1,0:T(4,128)S(1)}, u32[]{:S(2)}) copy-start(f32[4,1024]{1,0:T(4,128)S(1)} %broadcast_multiply_fusion) | copy-start | bytes 49156
  13.8 4.4 copy-start.24
  13.8 453.3 %copy-start.22 = (f32[4,1024]{1,0:T(4,128)}, f32[4,1024]{1,0:T(4,128)S(1)}, u32[]{:S(2)}) copy-start(f32[4,1024]{1,0:T(4,128)S(1)} %fusion.58) | copy-start | bytes 49156
  13.8 146.0 %copy-start.41 = (bf16[96,64]{0,1:T(8,128)(2,1)S(1)}, bf16[96,64]{0,1:T(8,128)(2,1)}, u32[]{:S(2)}) copy-start(bf16[96,64]{0,1:T(8,128)(2,1)} %param.30) | copy-start | bytes 36868
  13.8 160.5 %copy-start.38 = (bf16[64,160]{1,0:T(8,128)(2,1)S(1)}, bf16[64,160]{1,0:T(8,128)(2,1)}, u32[]{:S(2)}) copy-start(bf16[64,160]{1,0:T(8,128)(2,1)} %param.24) | copy-start | bytes 61444
  13.8 175.1 %copy-start.39 = (bf16[160,64]{0,1:T(8,128)(2,1)S(1)}, bf16[160,64]{0,1:T(8,128)(2,1)}, u32[]{:S(2)}) copy-start(bf16[160,64]{0,1:T(8,128)(2,1)} %param.29) | copy-start | bytes 61444
  18.2 185.8 %copy-start.26 = (f32[1280]{0:T(1024)S(1)}, f32[1280]{0:T(1024)}, u32[]{:S(2)}) copy-start(f32[1280]{0:T(1024)} %param.27) | copy-start | bytes 15364
  18.2 185.8 %copy-start.44 = (f32[1280]{0:T(1024)S(1)}, f32[1280]{0:T(1024)}, u32[]{:S(2)}) copy-start(f32[1280]{0:T(1024)} %param.28) | copy-start | bytes 15364
  18.2 140.5 %collective-permute-start = (bf16[4,1024,768]{2,1,0:T(8,128)(2,1)}, bf16[4,1024,768]{2,1,0:T(8,128)(2,1)}, u32[]{:S(2)}, u32[]{:S(2)}) collective-permute-start(bf16[4,1024,768]{2,1,0:T(8,128)(2,1)} %fusion.22), channel_id=1, source_target_pairs={{0,1},{1,2},{2,3},{3,0},{4,5},{5,6},{6,7},{7,4},{8,9},{9,10},{10,1... | collective-permute-start | bytes 18874376 | tf_op jit(solution)/shard_map/ppermute | solution.py:25
  21.1 450.9 %collective-permute-start.2 = (bf16[4,1024,768]{2,1,0:T(8,128)(2,1)}, bf16[4,1024,768]{2,1,0:T(8,128)(2,1)}, u32[]{:S(2)}, u32[]{:S(2)}) collective-permute-start(bf16[4,1024,768]{2,1,0:T(8,128)(2,1)} %fusion.22), channel_id=1, source_target_pairs={{1,0},{2,1},{3,2},{0,3},{5,4},{6,5},{7,6},{4,7},{9,8},{10,9},{11,1... | collective-permute-start | bytes 18874376 | tf_op jit(solution)/shard_map/ppermute | solution.py:27
  158.7 313.3 %collective-permute-start.1 = (bf16[4,1024,768]{2,1,0:T(8,128)(2,1)}, bf16[4,1024,768]{2,1,0:T(8,128)(2,1)}, u32[]{:S(2)}, u32[]{:S(2)}) collective-permute-start(bf16[4,1024,768]{2,1,0:T(8,128)(2,1)} %collective-permute-done), channel_id=1, source_target_pairs={{0,1},{1,2},{2,3},{3,0},{4,5},{5,6},{6,7},{7,4},{8,9},{9,10},{10,1... | collective-permute-start | bytes 18874376 | tf_op jit(solution)/shard_map/ppermute | solution.py:25
  174.2 259.3 %copy-start.34 = (bf16[96,320]{1,0:T(8,128)(2,1)S(1)}, bf16[96,320]{1,0:T(8,128)(2,1)}, u32[]{:S(2)}) copy-start(bf16[96,320]{1,0:T(8,128)(2,1)} %param.31) | copy-start | bytes 184324
  174.3 398.4 %copy-start.17 = (bf16[768,64,1]{0,1,2:T(8,128)(2,1)}, bf16[768,64,1]{0,1,2:T(8,128)(2,1)S(1)}, u32[]{:S(2)}) copy-start(bf16[768,64,1]{0,1,2:T(8,128)(2,1)S(1)} %reshape.326) | copy-start | bytes 294916
  188.7 260.5 %copy-start.28 = (bf16[320,160]{0,1:T(8,128)(2,1)S(1)}, bf16[320,160]{0,1:T(8,128)(2,1)}, u32[]{:S(2)}) copy-start(bf16[320,160]{0,1:T(8,128)(2,1)} %param.32) | copy-start | bytes 307204
  188.9 278.1 %copy-start.3 = (f32[1280,64]{0,1:T(8,128)}, f32[1280,64]{0,1:T(8,128)S(1)}, u32[]{:S(2)}) copy-start(f32[1280,64]{0,1:T(8,128)S(1)} %reshape.324) | copy-start | bytes 983044
  203.6 268.4 %copy-start.13 = (bf16[1280,64]{0,1:T(8,128)(2,1)}, bf16[1280,64]{0,1:T(8,128)(2,1)S(1)}, u32[]{:S(2)}) copy-start(bf16[1280,64]{0,1:T(8,128)(2,1)S(1)} %reshape.323) | copy-start | bytes 491524
  203.8 268.2 %copy-start.42 = (f32[64]{0:T(128)}, f32[64]{0:T(128)S(1)}, u32[]{:S(2)}) copy-start(f32[64]{0:T(128)S(1)} %broadcast_multiply_fusion.2) | copy-start | bytes 772
  204.0 268.0 %copy-start.50 = (f32[64]{0:T(128)}, f32[64]{0:T(128)S(1)}, u32[]{:S(2)}) copy-start(f32[64]{0:T(128)S(1)} %multiply_reduce_fusion.3) | copy-start | bytes 772
  204.0 268.0 %copy-start.47 = (f32[64]{0:T(128)}, f32[64]{0:T(128)S(1)}, u32[]{:S(2)}) copy-start(f32[64]{0:T(128)S(1)} %fusion.62) | copy-start | bytes 772
  433.5 15.6 copy-start.7
  448.8 139.7 %copy-start.11 = (bf16[768,320]{1,0:T(8,128)(2,1)}, bf16[768,320]{1,0:T(8,128)(2,1)S(1)}, u32[]{:S(2)}) copy-start(bf16[768,320]{1,0:T(8,128)(2,1)S(1)} %all_gather.34) | copy-start | bytes 1474564
  588.5 17.0 %copy-start.52 = (s32[4]{0:T(128)S(1)}, s32[4]{0:T(128)}, u32[]{:S(2)}) copy-start(s32[4]{0:T(128)} %param.23) | copy-start | bytes 52
  605.5 50.5 %copy-start.9 = (bf16[320,1280]{0,1:T(8,128)(2,1)S(1)}, bf16[320,1280]{0,1:T(8,128)(2,1)}, u32[]{:S(2)}) copy-start(bf16[320,1280]{0,1:T(8,128)(2,1)} %all_gather.38) | copy-start | bytes 2457604
  656.0 5.4 copy-start.6
  661.5 62.4 %copy-start.4 = (f32[1280,64]{0,1:T(8,128)S(1)}, f32[1280,64]{0,1:T(8,128)}, u32[]{:S(2)}) copy-start(f32[1280,64]{0,1:T(8,128)} %copy-done.3) | copy-start | bytes 983044
  661.5 65.8 %copy-start.33 = (f32[1280]{0:T(1024)S(1)}, f32[1280]{0:T(1024)}, u32[]{:S(2)}) copy-start(f32[1280]{0:T(1024)} %param.33) | copy-start | bytes 15364
  661.5 65.7 %copy-start.45 = (f32[1280]{0:T(1024)S(1)}, f32[1280]{0:T(1024)}, u32[]{:S(2)}) copy-start(f32[1280]{0:T(1024)} %param.34) | copy-start | bytes 15364
  661.5 106.7 %all-gather.7.cloned.1.call-start = ((), (), s32[]{:S(2)}) async-start(), calls=%async_computation.13 | async-start | bytes 3276800 | tf_op jit(solution)/shard_map/all_gather | solution.py:163
  723.9 3.4 copy-start.5
  728.4 19.0 %copy-start.30 = (bf16[320,160]{0,1:T(8,128)(2,1)S(1)}, bf16[320,160]{0,1:T(8,128)(2,1)}, u32[]{:S(2)}) copy-start(bf16[320,160]{0,1:T(8,128)(2,1)} %param.37) | copy-start | bytes 307204
  728.5 81.3 %all-gather.9.cloned.1.call-start = ((), (), s32[]{:S(2)}) async-start(), calls=%async_computation.15 | async-start | bytes 3276800 | tf_op jit(solution)/shard_map/all_gather | solution.py:164
  729.4 151.6 %reduce-scatter.23.cloned.1.call-start = ((), (), s32[]{:S(2)}) async-start(), calls=%async_computation.16 | async-start | bytes 6553600 | tf_op jit(solution)/shard_map/reduce_scatter | solution.py:194
  809.7 5.8 copy-start.10
  819.5 104.0 %reduce-scatter.21.cloned.1.call-start = ((), (), s32[]{:S(2)}) async-start(), calls=%async_computation.14 | async-start | bytes 3276800 | tf_op jit(solution)/shard_map/reduce_scatter | solution.py:176
  824.0 99.5 %copy-start.46 = (f32[1280]{0:T(1024)S(1)}, f32[1280]{0:T(1024)}, u32[]{:S(2)}) copy-start(f32[1280]{0:T(1024)} %param.38) | copy-start | bytes 15364
  824.0 144.3 %all-gather.11.cloned.1.call-start = ((), (), s32[]{:S(2)}) async-start(), calls=%async_computation.17 | async-start | bytes 3276800 | tf_op jit(solution)/shard_map/all_gather | solution.py:198
  928.5 288.6 %reduce-scatter.27.cloned.1.call-start = ((), (), s32[]{:S(2)}) async-start(), calls=%async_computation.19 | async-start | bytes 819200 | tf_op jit(solution)/shard_map/reduce_scatter | solution.py:224
  972.2 174.5 %copy-start.14 = (bf16[1280,64]{0,1:T(8,128)(2,1)S(1)}, bf16[1280,64]{0,1:T(8,128)(2,1)}, u32[]{:S(2)}) copy-start(bf16[1280,64]{0,1:T(8,128)(2,1)} %copy-done.13) | copy-start | bytes 491524
  978.4 3.2 copy-start.1
  1147.9 105.0 %reduce-scatter.35.cloned.1.call-start = ((), (), s32[]{:S(2)}) async-start(), calls=%async_computation.23 | async-start | bytes 1105920 | tf_op jit(solution)/shard_map/reduce_scatter | solution.py:252
  1152.7 101.9 %reduce-scatter.33.cloned.1.call-start = ((), (), s32[]{:S(2)}) async-start(), calls=%async_computation.22 | async-start | bytes 1105920 | tf_op jit(solution)/shard_map/reduce_scatter | solution.py:246
  1157.2 115.2 %reduce-scatter.41.cloned.1.call-start = ((), (), s32[]{:S(2)}) async-start(), calls=%async_computation.26 | async-start | bytes 221184
  1157.2 11.6 copy-start.12
  1193.9 109.4 %reduce-scatter.39.cloned.1.call-start = ((), (), s32[]{:S(2)}) async-start(), calls=%async_computation.25 | async-start | bytes 368640
  1196.2 20.8 %copy-start.27 = (f32[1280]{0:T(1024)S(1)}, f32[1280]{0:T(1024)}, u32[]{:S(2)}) copy-start(f32[1280]{0:T(1024)} %param.27) | copy-start | bytes 15364
  1196.2 20.8 %copy-start.43 = (f32[64]{0:T(128)S(1)}, f32[64]{0:T(128)}, u32[]{:S(2)}) copy-start(f32[64]{0:T(128)} %copy-done.42) | copy-start | bytes 772
  1196.2 22.0 %copy-start.51 = (f32[64]{0:T(128)S(1)}, f32[64]{0:T(128)}, u32[]{:S(2)}) copy-start(f32[64]{0:T(128)} %copy-done.50) | copy-start | bytes 772
  1196.3 22.0 %copy-start.48 = (f32[64]{0:T(128)S(1)}, f32[64]{0:T(128)}, u32[]{:S(2)}) copy-start(f32[64]{0:T(128)} %copy-done.47) | copy-start | bytes 772
  1196.3 23.2 %copy-start.15 = (f32[64,1280]{1,0:T(8,128)S(1)}, f32[64,1280]{1,0:T(8,128)}, u32[]{:S(2)}) copy-start(f32[64,1280]{1,0:T(8,128)} %get-tuple-element.121) | copy-start | bytes 983044
  1196.3 138.6 %reduce-scatter.29.cloned.1.call-start = ((), (), s32[]{:S(2)}) async-start(), calls=%async_computation.20 | async-start | bytes 663552 | tf_op jit(solution)/shard_map/reduce_scatter | solution.py:243
  1217.0 149.0 %reduce-scatter.37.cloned.1.call-start = ((), (), s32[]{:S(2)}) async-start(), calls=%async_computation.24 | async-start | bytes 368640
  1221.5 4.9 copy-start.18
  1221.5 177.2 %reduce-scatter.31.cloned.1.call-start = ((), (), s32[]{:S(2)}) async-start(), calls=%async_computation.21 | async-start | bytes 1105920 | tf_op jit(solution)/shard_map/reduce_scatter | solution.py:249
  1226.1 396.2 %reduce-scatter.25.cloned.1.call-start = ((), (), s32[]{:S(2)}) async-start(), calls=%async_computation.18 | async-start | bytes 31457280 | tf_op jit(solution)/shard_map/reduce_scatter | solution.py:227
  1252.1 370.2 %copy-start.20 = (f32[4,1024]{1,0:T(4,128)S(1)}, f32[4,1024]{1,0:T(4,128)}, u32[]{:S(2)}) copy-start(f32[4,1024]{1,0:T(4,128)} %copy-done.19) | copy-start | bytes 49156
  1252.1 370.2 %copy-start.32 = (f32[768]{0:T(1024)S(1)}, f32[768]{0:T(1024)}, u32[]{:S(2)}) copy-start(f32[768]{0:T(1024)} %param.25) | copy-start | bytes 9220
  1400.4 229.7 %copy-start.25 = (f32[4,1024]{1,0:T(4,128)S(1)}, f32[4,1024]{1,0:T(4,128)}, u32[]{:S(2)}) copy-start(f32[4,1024]{1,0:T(4,128)} %copy-done.24) | copy-start | bytes 49156
  1400.4 229.7 %copy-start.23 = (f32[4,1024]{1,0:T(4,128)S(1)}, f32[4,1024]{1,0:T(4,128)}, u32[]{:S(2)}) copy-start(f32[4,1024]{1,0:T(4,128)} %copy-done.22) | copy-start | bytes 49156
  1622.3 7.8 copy-start.2
  1630.1 9.2 copy-start.35
  1630.1 9.2 copy-start.36
  1630.1 9.2 copy-start.37
  (10 other events, 22.2 us)
Sparse Core Ops, SparseCore 0:
  661.6 62.2 reduce-scatter.18
  728.6 39.6 all-gather.6
  770.1 39.6 all-gather.8
  819.6 61.4 reduce-scatter.22
  883.9 39.5 reduce-scatter.20
  928.6 39.6 all-gather.10
  1148.0 25.3 reduce-scatter.26
  1175.9 31.9 reduce-scatter.34
  1210.2 30.5 reduce-scatter.32
  1243.5 28.7 reduce-scatter.40
  1274.6 28.6 reduce-scatter.38
  1305.5 29.2 reduce-scatter.28
  1337.2 28.6 reduce-scatter.36
  1368.7 30.0 reduce-scatter.30
  1402.0 220.2 reduce-scatter.24
